TPU v7x, 128 devices: a whole 4x4x4 slice. The times are simulated.
128 devices in a mesh: seq: 32 (over y, x, z_lo), dp: 4 (over z_hi, core).
Axes of the slice: x: 4, y: 4, z: 4 (z_hi: 2, z_lo: 2; z = z_hi * 2 + z_lo), core: 2. Of those that a mesh axis runs over, the one named last changes fastest.
Arguments:
- queries: bfloat16 [4, 32, 1024, 1024], P('dp', 'seq'), may hold values from -6 to 6
- keys: bfloat16 [4, 32, 1024, 1024], P('dp', 'seq'), may hold values from -6 to 6
- values: bfloat16 [4, 32, 1024, 1024], P('dp', 'seq'), may hold values from -6 to 6
- out_weight: bfloat16 [1024, 2048], P(('seq', 'dp')), may hold values from -0.1875 to 0.1875
- cotangent: bfloat16 [4, 32, 1024, 2048], P('dp', 'seq'), may hold values from -6 to 6
Outputs:
- layer_out: bfloat16 [4, 32, 1024, 2048], P('dp', 'seq')
- query_grad: bfloat16 [4, 32, 1024, 1024], P('dp', 'seq')
- key_grad: bfloat16 [4, 32, 1024, 1024], P('dp', 'seq')
- value_grad: bfloat16 [4, 32, 1024, 1024], P('dp', 'seq')
- weight_grad: float32 [1024, 2048], P(('seq', 'dp'))
All inputs are finite; a program needn't handle non-finite values.
Results may differ from a plain program's by a relative error of at most 0.0071.
Values may be sent and summed in bfloat16 or wider, within the bound.
A program may use at most 128 MiB of HBM per device.

v0:
```python
import math

import jax
import jax.numpy as jnp
from jax import lax
from jax.sharding import PartitionSpec as P

ROW_HEADS = 4
COL_HEADS = 4
DH = 128


def attend_sets(query_set, key_set, value_set, upstream_set):
    factor = 1.0 / math.sqrt(query_set.shape[-1])
    scores = (
        jnp.einsum("...ld,...md->...lm", query_set, key_set, preferred_element_type=jnp.float32)
        * factor
    )
    length = scores.shape[-1]
    masked_out = lax.broadcasted_iota(jnp.int32, (length, length), 1) > lax.broadcasted_iota(
        jnp.int32, (length, length), 0
    )
    scores = jnp.where(masked_out, -jnp.inf, scores)
    peak_score = jnp.max(scores, axis=-1, keepdims=True)
    raised = jnp.exp(scores - peak_score)
    shares = raised / jnp.sum(raised, axis=-1, keepdims=True)
    shares_low = shares.astype(jnp.bfloat16)
    output = jnp.einsum(
        "...lm,...md->...ld", shares_low, value_set, preferred_element_type=jnp.float32
    ).astype(jnp.bfloat16)
    share_grad = jnp.einsum(
        "...ld,...md->...lm", upstream_set, value_set, preferred_element_type=jnp.float32
    )
    value_grad = jnp.einsum(
        "...lm,...ld->...md", shares_low, upstream_set, preferred_element_type=jnp.float32
    ).astype(jnp.bfloat16)
    row_total = jnp.sum(shares * share_grad, axis=-1, keepdims=True)
    score_low = (shares * (share_grad - row_total)).astype(jnp.bfloat16)
    query_grad = (
        jnp.einsum("...lm,...md->...ld", score_low, key_set, preferred_element_type=jnp.float32)
        * factor
    ).astype(jnp.bfloat16)
    key_grad = (
        jnp.einsum("...lm,...ld->...md", score_low, query_set, preferred_element_type=jnp.float32)
        * factor
    ).astype(jnp.bfloat16)
    return (output, query_grad, key_grad, value_grad)


def group_step(grouped):
    return attend_sets(grouped[0], grouped[1], grouped[2], grouped[3])


def column_sets(gathered):
    reordered = [jnp.moveaxis(member, 1, 3) for member in gathered]
    results = attend_sets(reordered[0], reordered[1], reordered[2], reordered[3])
    return tuple((jnp.moveaxis(member, 3, 1) for member in results))


def body(queries, keys, values, out_weight, cotangent):
    seq_count, rows_here, stride, head_width = queries.shape
    model_width = cotangent.shape[-1]
    row_width = ROW_HEADS * DH
    flat_cot = cotangent.reshape(-1, model_width)
    weight_full = lax.all_gather(out_weight, ("seq", "dp"), axis=0, tiled=True)
    upstream_wide = jnp.einsum(
        "td,hd->th", flat_cot, weight_full, preferred_element_type=jnp.float32
    )
    upstream = upstream_wide.astype(jnp.bfloat16).reshape(seq_count, rows_here, stride, head_width)

    def column_part(member):
        return member[..., row_width:].reshape(seq_count, rows_here, stride, COL_HEADS, DH)

    column_query = column_part(queries)
    column_key = column_part(keys)
    column_value = column_part(values)
    column_upstream = column_part(upstream)
    column_output, column_qgrad, column_kgrad, column_vgrad = column_sets(
        (
            lax.all_to_all(column_query, "seq", split_axis=2, concat_axis=1, tiled=True),
            lax.all_to_all(column_key, "seq", split_axis=2, concat_axis=1, tiled=True),
            lax.all_to_all(column_value, "seq", split_axis=2, concat_axis=1, tiled=True),
            lax.all_to_all(column_upstream, "seq", split_axis=2, concat_axis=1, tiled=True),
        )
    )

    def row_part(member):
        return jnp.moveaxis(
            member[..., :row_width].reshape(seq_count, rows_here, stride, ROW_HEADS, DH), 3, 0
        )

    row_results = lax.map(
        group_step, (row_part(queries), row_part(keys), row_part(values), row_part(upstream))
    )
    row_layout = (
        lax.all_to_all(column_output, "seq", split_axis=1, concat_axis=2, tiled=True),
        lax.all_to_all(column_qgrad, "seq", split_axis=1, concat_axis=2, tiled=True),
        lax.all_to_all(column_kgrad, "seq", split_axis=1, concat_axis=2, tiled=True),
        lax.all_to_all(column_vgrad, "seq", split_axis=1, concat_axis=2, tiled=True),
    )
    joined = []
    for row_member, col_member in zip(row_results, row_layout):
        row_flat = jnp.moveaxis(row_member, 0, 3).reshape(seq_count, rows_here, stride, row_width)
        col_flat = col_member.reshape(seq_count, rows_here, stride, COL_HEADS * DH)
        joined.append(jnp.concatenate([row_flat, col_flat], axis=-1))
    attn_flat = joined[0].reshape(-1, head_width)
    projected = jnp.dot(attn_flat, weight_full, preferred_element_type=jnp.float32)
    layer_out = projected.astype(jnp.bfloat16).reshape(seq_count, rows_here, stride, model_width)
    seq_devices = lax.axis_size("seq")
    dp_devices = lax.axis_size("dp")
    token_total = seq_count * dp_devices * rows_here * seq_devices * stride
    grad_factor = 1.0 / math.sqrt(token_total)
    weight_grad = lax.psum_scatter(
        jnp.einsum("th,td->hd", attn_flat, flat_cot, preferred_element_type=jnp.float32)
        * grad_factor,
        ("seq", "dp"),
        scatter_dimension=0,
        tiled=True,
    )
    return (layer_out, joined[1], joined[2], joined[3], weight_grad)


def solution(mesh):
    return jax.shard_map(
        body,
        mesh=mesh,
        in_specs=(
            P("dp", "seq", None, None),
            P("dp", "seq", None, None),
            P("dp", "seq", None, None),
            P(("seq", "dp"), None),
            P("dp", "seq", None, None),
        ),
        out_specs=(
            P("dp", "seq", None, None),
            P("dp", "seq", None, None),
            P("dp", "seq", None, None),
            P("dp", "seq", None, None),
            P(("seq", "dp"), None),
        ),
        check_vma=False,
    )
```

profile of v0, /device:TPU:1, one launch (start us, length us, event | category | flops | bytes accessed | tf_op | source)
XLA Modules:
  0.0 981.5 jit_solution(38940952520607653)
XLA Ops:
  7.9 2.7 fusion.93
  12.5 9.2 all-to-all-start
  21.8 2.6 fusion.92
  26.4 13.8 %all-to-all-done = bf16[1,1,1024,4,128]{4,3,1,0,2:T(4,128)(2,1)S(1)} async-done(((bf16[1,1,1024,4,128]{4,3,1,0,2:T(4,128)(2,1)}), bf16[1,1,1024,4,128]{4,3,1,0,2:T(4,128)(2,1)S(1)}, u32[]{:S(2)}, u32[]{:S(2)}) %all-to-all-start) | async-done | bytes 1048608 | tf_op jit(solution)/shard_map/all_to_all | solution.py:80
  40.2 3.9 all-to-all-start.1
  44.1 3.0 fusion.91
  50.1 11.5 %all-to-all-done.1 = bf16[1,1,1024,4,128]{4,3,1,0,2:T(4,128)(2,1)S(1)} async-done(((bf16[1,1,1024,4,128]{4,3,1,0,2:T(4,128)(2,1)}), bf16[1,1,1024,4,128]{4,3,1,0,2:T(4,128)(2,1)S(1)}, u32[]{:S(2)}, u32[]{:S(2)}) %all-to-all-start.1) | async-done | bytes 1048608 | tf_op jit(solution)/shard_map/all_to_all | solution.py:81
  61.6 3.9 all-to-all-start.2
  65.5 3.2 fusion.94
  68.8 12.6 %all-to-all-done.2 = bf16[1,1,1024,4,128]{4,3,1,0,2:T(4,128)(2,1)S(1)} async-done(((bf16[1,1,1024,4,128]{4,3,1,0,2:T(4,128)(2,1)}), bf16[1,1,1024,4,128]{4,3,1,0,2:T(4,128)(2,1)S(1)}, u32[]{:S(2)}, u32[]{:S(2)}) %all-to-all-start.2) | async-done | bytes 1048608 | tf_op jit(solution)/shard_map/all_to_all | solution.py:82
  82.4 2.5 fusion.47
  86.5 4.5 all-to-all-start.3
  96.5 10.0 %all-to-all-done.3 = bf16[1,32,32,4,128]{4,3,2,0,1:T(4,128)(2,1)S(1)} async-done(((bf16[1,32,32,4,128]{4,3,2,0,1:T(4,128)(2,1)}), bf16[1,32,32,4,128]{4,3,2,0,1:T(4,128)(2,1)S(1)}, u32[]{:S(2)}, u32[]{:S(2)}) %all-to-all-start.3) | async-done | bytes 1048608 | tf_op jit(solution)/shard_map/all_to_all | solution.py:96
  107.5 120.6 %all-gather.2.cloned.1.call-done = bf16[1024,2048]{1,0:T(8,128)(2,1)} async-done(((bf16[8,2048]{1,0:T(8,128)(2,1)}), bf16[1024,2048]{1,0:T(8,128)(2,1)}) %all-gather.2.cloned.1.call-update) | async-done | bytes 4194320 | tf_op jit(solution)/shard_map/all_gather | solution.py:65
  228.1 8.0 convert_bitcast_fusion.1
  237.6 72.4 %while.16 = (s32[]{:T(128)}, bf16[4,1,1,1024,128]{3,4,0,2,1:T(8,128)(2,1)}, bf16[4,1,1,1024,128]{4,3,2,1,0:T(8,128)(2,1)}, bf16[4,1,1,1024,128]{4,3,2,1,0:T(8,12...) while((s32[]{:T(128)}, ...), condition=%wide.region_4.5_spmd, body=%wide.region_0.4_spmd.sunk | while | flops 1649144832 | bytes 77653160 | solution.py:92
  244.1 3.8 fusion.135
  262.1 3.8 fusion.135
  280.2 3.8 fusion.135
  298.2 3.8 fusion.135
  310.0 10.3 %convolution_multiply_fusion.2 = f32[1024,2048]{1,0:T(8,128)} fusion(bf16[1,1,1024,2048]{3,2,1,0:T(8,128)(2,1)} %param.11, bf16[1,1,1024,512]{2,3,1,0:T(8,128)(2,1)S(1)} %copy.90, bf16[1,1,1024,512]{2,3,1,0:T(8,128)(2,1)} %bitcast.226), kind=kOutput, calls=%fused_computation.49 | convolution fusion | flops 4301258752 | bytes 14680064 | tf_op jit(solution)/shard_map/th,td->hd/dot_general | solution.py:114
  321.0 22.4 %all_to_all.84 = bf16[1,1,1024,4,128]{4,3,1,0,2:T(4,128)(2,1)S(1)} all-to-all(bf16[1,1,1024,4,128]{4,3,1,0,2:T(4,128)(2,1)S(1)} %copy.92), channel_id=1, replica_groups=mesh['seq'=32,'dp'=4] {'seq'}, dimensions={2} | all-to-all | bytes 2097152 | tf_op jit(solution)/shard_map/all_to_all | solution.py:83
  343.5 2.8 fusion.48
  347.9 4.3 all-to-all-start.7
  352.2 3.4 multiply_reduce_fusion.1
  359.2 8.1 all-to-all-done.7
  367.3 5.8 all-to-all-start.6
  380.2 7.4 all-to-all-done.6
  387.6 5.5 all-to-all-start.5
  395.5 9.1 convert_bitcast_fusion
  409.4 3.0 pad_maximum_fusion.2
  415.6 558.8 %reduce-scatter.2.cloned.1.call-done = f32[8,2048]{1,0:T(8,128)} async-done(((f32[1024,2048]{1,0:T(8,128)}), f32[8,2048]{1,0:T(8,128)}) %reduce-scatter.2.cloned.1.call-update) | async-done | bytes 65552 | tf_op jit(solution)/shard_map/reduce_scatter | solution.py:113
  (129 shorter events, 98.1 us)
Async XLA Ops:
  7.2 220.9 %all-gather.2.cloned.1.call-start = ((), (), s32[]{:S(2)}) async-start(), calls=%async_computation.9 | async-start | bytes 4227072 | tf_op jit(solution)/shard_map/all_gather | solution.py:65
  12.5 27.7 %all-to-all-start = ((bf16[1,1,1024,4,128]{4,3,1,0,2:T(4,128)(2,1)}), bf16[1,1,1024,4,128]{4,3,1,0,2:T(4,128)(2,1)S(1)}, u32[]{:S(2)}, u32[]{:S(2)}) async-start(bf16[1,1,1024,4,128]{4,3,1,0,2:T(4,128)(2,1)} %copy.77), calls=%async_computation | async-start | bytes 2097152 | tf_op jit(solution)/shard_map/all_to_all | solution.py:80
  40.2 25.3 %copy-start.4 = (bf16[1,1,1024,4,128]{4,3,1,0,2:T(4,128)(2,1)}, bf16[1,1,1024,4,128]{4,3,1,0,2:T(4,128)(2,1)S(1)}, u32[]{:S(2)}) copy-start(bf16[1,1,1024,4,128]{4,3,1,0,2:T(4,128)(2,1)S(1)} %all-to-all-done) | copy-start | bytes 3145732
  40.2 21.4 %all-to-all-start.1 = ((bf16[1,1,1024,4,128]{4,3,1,0,2:T(4,128)(2,1)}), bf16[1,1,1024,4,128]{4,3,1,0,2:T(4,128)(2,1)S(1)}, u32[]{:S(2)}, u32[]{:S(2)}) async-start(bf16[1,1,1024,4,128]{4,3,1,0,2:T(4,128)(2,1)} %copy.81), calls=%async_computation.1 | async-start | bytes 2097152 | tf_op jit(solution)/shard_map/all_to_all | solution.py:81
  61.6 7.2 copy-start.2
  61.6 19.9 %all-to-all-start.2 = ((bf16[1,1,1024,4,128]{4,3,1,0,2:T(4,128)(2,1)}), bf16[1,1,1024,4,128]{4,3,1,0,2:T(4,128)(2,1)S(1)}, u32[]{:S(2)}, u32[]{:S(2)}) async-start(bf16[1,1,1024,4,128]{4,3,1,0,2:T(4,128)(2,1)} %copy.85), calls=%async_computation.2 | async-start | bytes 2097152 | tf_op jit(solution)/shard_map/all_to_all | solution.py:82
  68.8 167.3 %copy-start.19 = (f32[32,4,32]{2,1,0:T(4,128)}, f32[32,4,32]{2,1,0:T(4,128)S(1)}, u32[]{:S(2)}) copy-start(f32[32,4,32]{2,1,0:T(4,128)S(1)} %get-tuple-element.116) | copy-start | bytes 49156
  85.0 6.6 copy-start.6
  85.0 7.9 copy-start.7
  86.5 20.0 %all-to-all-start.3 = ((bf16[1,32,32,4,128]{4,3,2,0,1:T(4,128)(2,1)}), bf16[1,32,32,4,128]{4,3,2,0,1:T(4,128)(2,1)S(1)}, u32[]{:S(2)}, u32[]{:S(2)}) async-start(bf16[1,32,32,4,128]{4,3,2,0,1:T(4,128)(2,1)} %copy.89), calls=%async_computation.3 | async-start | bytes 2097152 | tf_op jit(solution)/shard_map/all_to_all | solution.py:96
  91.0 883.4 %reduce-scatter.2.cloned.1.call-start = ((), (), s32[]{:S(2)}) async-start(), calls=%async_computation.10 | async-start | bytes 8454144 | tf_op jit(solution)/shard_map/reduce_scatter | solution.py:113
  107.4 202.5 %copy-start.16 = (bf16[1,1,1024,512]{2,3,1,0:T(8,128)(2,1)}, bf16[1,1,1024,512]{2,3,1,0:T(8,128)(2,1)S(1)}, u32[]{:S(2)}) copy-start(bf16[1,1,1024,512]{2,3,1,0:T(8,128)(2,1)S(1)} %copy.90) | copy-start | bytes 3145732
  239.4 2.0 copy-start
  244.1 3.8 copy-start.1
  257.4 2.0 copy-start
  262.1 3.8 copy-start.1
  280.2 3.8 copy-start.1
  298.2 3.8 copy-start.1
  320.3 23.2 %copy-start.20 = (f32[32,4,32]{2,1,0:T(4,128)S(1)}, f32[32,4,32]{2,1,0:T(4,128)}, u32[]{:S(2)}) copy-start(f32[32,4,32]{2,1,0:T(4,128)} %copy-done.19) | copy-start | bytes 49156
  343.5 2.9 copy-start.18
  346.3 5.9 copy-start.13
  347.9 19.4 %all-to-all-start.7 = ((bf16[1,32,32,4,128]{4,3,2,0,1:T(4,128)(2,1)}), bf16[1,32,32,4,128]{4,3,2,0,1:T(4,128)(2,1)S(1)}, u32[]{:S(2)}, u32[]{:S(2)}) async-start(bf16[1,32,32,4,128]{4,3,2,0,1:T(4,128)(2,1)} %copy.100), calls=%async_computation.7 | async-start | bytes 2097152 | tf_op jit(solution)/shard_map/all_to_all | solution.py:99
  352.2 3.4 copy-start.14
  357.7 20.0 %copy-start.3 = (bf16[1,1,1024,4,128]{4,3,1,0,2:T(4,128)(2,1)S(1)}, bf16[1,1,1024,4,128]{4,3,1,0,2:T(4,128)(2,1)}, u32[]{:S(2)}) copy-start(bf16[1,1,1024,4,128]{4,3,1,0,2:T(4,128)(2,1)} %copy-done.2) | copy-start | bytes 3145732
  367.3 20.4 %all-to-all-start.6 = ((bf16[1,32,32,4,128]{4,3,2,0,1:T(4,128)(2,1)}), bf16[1,32,32,4,128]{4,3,2,0,1:T(4,128)(2,1)}, u32[]{:S(2)}, u32[]{:S(2)}) async-start(bf16[1,32,32,4,128]{4,3,2,0,1:T(4,128)(2,1)} %copy.98), calls=%async_computation.6 | async-start | bytes 2097152 | tf_op jit(solution)/shard_map/all_to_all | solution.py:98
  378.7 16.9 %copy-start.17 = (bf16[1,1,1024,512]{2,3,1,0:T(8,128)(2,1)S(1)}, bf16[1,1,1024,512]{2,3,1,0:T(8,128)(2,1)}, u32[]{:S(2)}) copy-start(bf16[1,1,1024,512]{2,3,1,0:T(8,128)(2,1)} %copy-done.16) | copy-start | bytes 3145732
  387.6 20.6 %all-to-all-start.5 = ((bf16[1,32,32,4,128]{4,3,2,0,1:T(4,128)(2,1)}), bf16[1,32,32,4,128]{4,3,2,0,1:T(4,128)(2,1)S(1)}, u32[]{:S(2)}, u32[]{:S(2)}) async-start(bf16[1,32,32,4,128]{4,3,2,0,1:T(4,128)(2,1)} %copy.96), calls=%async_computation.5 | async-start | bytes 2097152 | tf_op jit(solution)/shard_map/all_to_all | solution.py:97
  404.6 4.8 copy-start.9
  405.9 6.5 copy-start.10
  409.4 3.0 copy-start.11
  409.4 4.6 copy-start.8
  409.4 4.6 copy-start.12
  (4 other events, 6.3 us)
Sparse Core Ops, SparseCore 0:
  9.7 218.3 all-gather.1
  320.4 654.0 reduce-scatter.1
where the time goes:
time: 992 us; the launch traced here: 982 us
  waiting for transfers between devices  744 us (75%)
  matrix products  97.7 us (10%)
  local copies, waits for them, and re-layouts  52.1 us (5%)
  starting transfers between devices  37.8 us (4%)
  blocking collectives  22.4 us (2%)
  between operations  14.6 us (1%)
  other arithmetic  13 us (1%)
    reduce_scatter x1, waiting for transfers between devices, body(): lax.psum_scatter(jnp.einsum('th,td->hd', attn_flat, flat_cot, preferred_e...  559 us
    all_gather x1, waiting for transfers between devices, body(): weight_full = lax.all_gather(out_weight, ('seq', 'dp'), axis=0, tiled=True)  121 us
    all_to_all x1, blocking collectives, body(): lax.all_to_all(column_upstream, 'seq', split_axis=2, concat_axis=1, tiled...  22.4 us
  transfers between devices with their start and end apart: 9, of which 8 were waited for; matrix products, arithmetic and copies ran while one was open for 7% of the time, Pallas kernels for 0%

commit v1 on v0

v1 whole, which is shorter than its diff:
```python
import functools
import math

import jax
import jax.numpy as jnp
from jax import lax
from jax.experimental import pallas as pl
from jax.experimental.pallas import tpu as pltpu
from jax.sharding import PartitionSpec as P

ROW_HEADS = 4
COL_HEADS = 4
DH = 128
MESH = pl.DeviceIdType.MESH
VMEM_LIMIT = 67000000
PIECES = ((0, 384), (384, 384), (768, 256))
ORDERS = ((2, 1, 0), (1, 0, 2), (0, 2, 1))


def place():
    s = lax.axis_index("seq")
    p = lax.axis_index("dp")
    return (s // 8, (s // 2) % 4, (s % 2) * 2 + p // 2), p % 2


def device(at, core):
    y, x, z = at
    return ((y * 4 + x) * 2 + z // 2, (z % 2) * 2 + core)


def shifted(at, axis, step):
    moved = list(at)
    moved[axis] = (at[axis] + step) % 4
    return tuple(moved)


def greet(seq_peers, ring_peers):
    s = lax.axis_index("seq")
    p = lax.axis_index("dp")
    at, core = place()
    barrier = pltpu.get_barrier_semaphore()
    count = 0
    if seq_peers:

        @pl.loop(1, 32)
        def _(k):
            pl.semaphore_signal(
                barrier, inc=1, device_id=((s + k) % 32, p), device_id_type=MESH
            )

        count += 31
    if ring_peers:
        pl.semaphore_signal(barrier, inc=1, device_id=device(at, 1 - core), device_id_type=MESH)
        count += 1
        for axis in range(3):
            for step in range(1, 4):
                pl.semaphore_signal(
                    barrier,
                    inc=1,
                    device_id=device(shifted(at, axis, step), core),
                    device_id_type=MESH,
                )
                count += 1
    pl.semaphore_wait(barrier, count)


def remote(src, dst, send, recv, to):
    return pltpu.make_async_remote_copy(
        src_ref=src, dst_ref=dst, send_sem=send, recv_sem=recv, device_id=to, device_id_type=MESH
    )


def wait_bytes(ref, sem):
    pltpu.make_async_copy(ref, ref, sem).wait()


def gather_weight(w_ref, pair, full, send, recv, local):
    at, core = place()
    other = device(at, 1 - core)
    swap = remote(w_ref, pair.at[core], send.at[0], recv.at[0], other)
    swap.start()
    own = pltpu.make_async_copy(w_ref, pair.at[core], local)
    own.start()
    own.wait()
    swap.wait()
    half = core * 1024
    own_half = pl.ds(pl.multiple_of(half, 128), 1024)
    full[at[0], at[1], at[2], :, own_half] = jnp.concatenate(
        [pair[0, :, own_half], pair[1, :, own_half]], axis=0
    )
    sem = 1
    for stage in range(3):
        for (start, width), order in zip(PIECES, ORDERS):
            index = tuple(
                pl.ds(0, 4) if axis in order[:stage] else at[axis] for axis in range(3)
            )
            cols = pl.ds(pl.multiple_of(half + start, 128), width)
            region = full.at[index + (slice(None), cols)]
            for step in range(1, 4):
                remote(
                    region,
                    region,
                    send.at[sem],
                    recv.at[sem],
                    device(shifted(at, order[stage], step), core),
                ).start()
            sem += 1
        for k, ((start, width), order) in enumerate(zip(PIECES, ORDERS)):
            index = tuple(
                pl.ds(0, 3)
                if axis == order[stage]
                else (pl.ds(0, 4) if axis in order[:stage] else at[axis])
                for axis in range(3)
            )
            got = full.at[index + (slice(None), pl.ds(0, width))]
            wait_bytes(got, recv.at[sem - 3 + k])
            wait_bytes(got, send.at[sem - 3 + k])
    mine = full.at[:, :, :, :, pl.ds(pl.multiple_of(half, 128), 1024)]
    last = remote(mine, mine, send.at[sem], recv.at[sem], other)
    last.start()
    last.wait()


def gather_kernel(w_ref, out_ref, pair, full, send, recv, local):
    greet(False, True)
    gather_weight(w_ref, pair, full, send, recv, local)
    out = pltpu.make_async_copy(full, out_ref, local)
    out.start()
    out.wait()


def scatter_grad(g_ref, out_ref, bufs, send, recv, factor):
    chip, firsts, seconds, thirds, sums1, sums2, fin, rest = bufs
    at, core = place()
    other = device(at, 1 - core)
    mine = pl.ds(pl.multiple_of(core * 1024, 128), 1024)
    theirs = pl.ds(pl.multiple_of((1 - core) * 1024, 128), 1024)
    swap = remote(g_ref.at[:, :, :, :, theirs], chip, send.at[0], recv.at[0], other)
    swap.start()
    swap.wait()

    @pl.loop(0, 4)
    def _(y):
        @pl.loop(0, 4)
        def _(x):
            total = chip[y, x].astype(jnp.float32) + g_ref[y, x, :, :, mine].astype(jnp.float32)
            chip[y, x] = total.astype(jnp.bfloat16)

    sem = 1
    for stage in range(3):
        for k, ((start, width), order) in enumerate(zip(PIECES, ORDERS)):
            path = order[::-1]
            axis = path[stage]
            left = [a for a in range(3) if a not in path[:stage]]
            for step in range(1, 4):
                to = shifted(at, axis, step)
                index = tuple(to[a] if a == axis else slice(None) for a in left)
                if stage == 0:
                    src = chip.at[index + (slice(None), pl.ds(start, width))]
                    dst = firsts[k].at[step - 1]
                elif stage == 1:
                    src = sums1[k].at[index]
                    dst = seconds[k].at[step - 1]
                else:
                    src = sums2[k].at[index]
                    dst = thirds[k].at[step - 1]
                remote(src, dst, send.at[sem], recv.at[sem], device(to, core)).start()
            sem += 1
        for k, ((start, width), order) in enumerate(zip(PIECES, ORDERS)):
            path = order[::-1]
            axis = path[stage]
            left = [a for a in range(3) if a not in path[:stage]]
            index = tuple(at[a] if a == axis else slice(None) for a in left)
            got = (firsts, seconds, thirds)[stage][k]
            wait_bytes(got, recv.at[sem - 3 + k])
            wait_bytes(got, send.at[sem - 3 + k])
            if stage == 0:
                own = chip[index + (slice(None), pl.ds(start, width))]
            elif stage == 1:
                own = sums1[k][index]
            else:
                own = sums2[k][index]
            total = own.astype(jnp.float32)
            for step in range(3):
                total = total + got[step].astype(jnp.float32)
            if stage == 0:
                sums1[k][...] = total.astype(jnp.bfloat16)
            elif stage == 1:
                sums2[k][...] = total.astype(jnp.bfloat16)
            else:
                for low in range(2):
                    fin[low, :, pl.ds(start, width)] = total[low * 8 : low * 8 + 8] * factor
    last = remote(fin.at[1 - core], rest, send.at[sem], recv.at[sem], other)
    last.start()
    last.wait()
    out_ref[:, mine] = fin[core]
    out_ref[:, theirs] = rest[...]


def scatter_bufs():
    def three(*lead):
        return [pltpu.VMEM(lead + (width,), jnp.bfloat16) for _, width in PIECES]

    return [
        pltpu.VMEM((4, 4, 4, 16, 1024), jnp.bfloat16),
        three(3, 4, 4, 16),
        three(3, 4, 16),
        three(3, 16),
        three(4, 4, 16),
        three(4, 16),
        pltpu.VMEM((2, 8, 1024), jnp.float32),
        pltpu.VMEM((8, 1024), jnp.float32),
    ]


def scatter_kernel(factor, g_ref, out_ref, bufs, send, recv):
    greet(False, True)
    scatter_grad(g_ref, out_ref, bufs, send, recv, factor)


def exchange_kernel(count, forward, *refs):
    xs, outs = refs[:count], refs[count : 2 * count]
    send, recv, local = refs[2 * count :]
    s = lax.axis_index("seq")
    p = lax.axis_index("dp")
    greet(True, False)
    half = pl.ds(512, 512)

    def src(t, q):
        return xs[t].at[pl.ds(q * 32, 32), half] if forward else xs[t].at[q]

    def dst(t):
        return outs[t].at[s] if forward else outs[t].at[pl.ds(s * 32, 32)]

    def some(t):
        return outs[t].at[pl.ds(0, 31)] if forward else outs[t].at[pl.ds(0, 31 * 32)]

    for t in range(count):

        @pl.loop(1, 32)
        def _(k):
            q = (s + k) % 32
            remote(src(t, q), dst(t), send.at[t], recv.at[t], (q, p)).start()

        pltpu.make_async_copy(src(t, s), dst(t), local.at[t]).start()
    for t in range(count):
        pltpu.make_async_copy(src(t, s), dst(t), local.at[t]).wait()
        wait_bytes(some(t), recv.at[t])
        wait_bytes(some(t), send.at[t])


ANY = pl.BlockSpec(memory_space=pl.ANY)
INV = pl.BlockSpec(memory_space=pltpu.VMEM)


def params(collective_id):
    return pltpu.CompilerParams(
        collective_id=collective_id, has_side_effects=True, vmem_limit_bytes=VMEM_LIMIT
    )


def all_weight(out_weight):
    full = pl.pallas_call(
        gather_kernel,
        out_shape=jax.ShapeDtypeStruct((4, 4, 4, 16, 2048), jnp.bfloat16),
        in_specs=[ANY],
        out_specs=ANY,
        scratch_shapes=[
            pltpu.VMEM((2, 8, 2048), jnp.bfloat16),
            pltpu.VMEM((4, 4, 4, 16, 2048), jnp.bfloat16),
            pltpu.SemaphoreType.DMA((11,)),
            pltpu.SemaphoreType.DMA((11,)),
            pltpu.SemaphoreType.DMA,
        ],
        compiler_params=params(1),
    )(out_weight)
    return full.reshape(1024, 2048)


def summed_grad(grad, factor):
    return pl.pallas_call(
        functools.partial(scatter_kernel, factor),
        out_shape=jax.ShapeDtypeStruct((8, 2048), jnp.float32),
        in_specs=[INV],
        out_specs=INV,
        scratch_shapes=[
            scatter_bufs(),
            pltpu.SemaphoreType.DMA((11,)),
            pltpu.SemaphoreType.DMA((11,)),
        ],
        compiler_params=params(2),
    )(grad.reshape(4, 4, 4, 16, 2048))


def exchange(arrays, forward, collective_id):
    shape = (32, 32, 512) if forward else (1024, 512)
    return pl.pallas_call(
        functools.partial(exchange_kernel, len(arrays), forward),
        out_shape=[jax.ShapeDtypeStruct(shape, jnp.bfloat16)] * len(arrays),
        in_specs=[ANY] * len(arrays),
        out_specs=[ANY] * len(arrays),
        scratch_shapes=[pltpu.SemaphoreType.DMA((len(arrays),))] * 3,
        compiler_params=params(collective_id),
    )(*arrays)


def attend_sets(query_set, key_set, value_set, upstream_set):
    factor = 1.0 / math.sqrt(query_set.shape[-1])
    scores = (
        jnp.einsum("...ld,...md->...lm", query_set, key_set, preferred_element_type=jnp.float32)
        * factor
    )
    length = scores.shape[-1]
    masked_out = lax.broadcasted_iota(jnp.int32, (length, length), 1) > lax.broadcasted_iota(
        jnp.int32, (length, length), 0
    )
    scores = jnp.where(masked_out, -jnp.inf, scores)
    peak_score = jnp.max(scores, axis=-1, keepdims=True)
    raised = jnp.exp(scores - peak_score)
    shares = raised / jnp.sum(raised, axis=-1, keepdims=True)
    shares_low = shares.astype(jnp.bfloat16)
    output = jnp.einsum(
        "...lm,...md->...ld", shares_low, value_set, preferred_element_type=jnp.float32
    ).astype(jnp.bfloat16)
    share_grad = jnp.einsum(
        "...ld,...md->...lm", upstream_set, value_set, preferred_element_type=jnp.float32
    )
    value_grad = jnp.einsum(
        "...lm,...ld->...md", shares_low, upstream_set, preferred_element_type=jnp.float32
    ).astype(jnp.bfloat16)
    row_total = jnp.sum(shares * share_grad, axis=-1, keepdims=True)
    score_low = (shares * (share_grad - row_total)).astype(jnp.bfloat16)
    query_grad = (
        jnp.einsum("...lm,...md->...ld", score_low, key_set, preferred_element_type=jnp.float32)
        * factor
    ).astype(jnp.bfloat16)
    key_grad = (
        jnp.einsum("...lm,...ld->...md", score_low, query_set, preferred_element_type=jnp.float32)
        * factor
    ).astype(jnp.bfloat16)
    return (output, query_grad, key_grad, value_grad)


def body(queries, keys, values, out_weight, cotangent):
    flat = [member.reshape(1024, 1024) for member in (queries, keys, values)]
    flat_cot = cotangent.reshape(1024, 2048)
    weight_full = all_weight(out_weight)
    upstream = jnp.einsum(
        "td,hd->th", flat_cot, weight_full, preferred_element_type=jnp.float32
    ).astype(jnp.bfloat16)
    members = flat + [upstream]
    columns = exchange(members, True, 3)
    columns = [jnp.moveaxis(member.reshape(32, 32, 4, 128), 0, 2) for member in columns]
    column_results = attend_sets(*columns)
    returned = exchange(
        [jnp.moveaxis(member, 2, 0).reshape(32, 32, 512) for member in column_results], False, 4
    )
    row_results = lax.map(
        lambda group: attend_sets(*group),
        tuple(
            jnp.moveaxis(member[:, :512].reshape(1024, 4, 128), 1, 0) for member in members
        ),
    )
    joined = [
        jnp.concatenate([jnp.moveaxis(row, 0, 1).reshape(1024, 512), col], axis=-1)
        for row, col in zip(row_results, returned)
    ]
    attn = joined[0]
    layer_out = jnp.dot(attn, weight_full, preferred_element_type=jnp.float32).astype(jnp.bfloat16)
    grad = jnp.einsum("th,td->hd", attn, flat_cot, preferred_element_type=jnp.float32)
    weight_grad = summed_grad(grad.astype(jnp.bfloat16), 1.0 / math.sqrt(4 * 32 * 1024))
    return (
        layer_out.reshape(1, 1, 1024, 2048),
        joined[1].reshape(1, 1, 1024, 1024),
        joined[2].reshape(1, 1, 1024, 1024),
        joined[3].reshape(1, 1, 1024, 1024),
        weight_grad,
    )


def solution(mesh):
    return jax.shard_map(
        body,
        mesh=mesh,
        in_specs=(
            P("dp", "seq", None, None),
            P("dp", "seq", None, None),
            P("dp", "seq", None, None),
            P(("seq", "dp"), None),
            P("dp", "seq", None, None),
        ),
        out_specs=(
            P("dp", "seq", None, None),
            P("dp", "seq", None, None),
            P("dp", "seq", None, None),
            P("dp", "seq", None, None),
            P(("seq", "dp"), None),
        ),
        check_vma=False,
    )
```

time: 992 us -> 282 us (0.28); the launches traced: 982 us -> 282 us
  waiting for transfers between devices: 744 us -> 0 us
  Pallas kernels: 0 us -> 173 us
  starting transfers between devices: 37.8 us -> 0 us
  matrix products: 97.7 us -> 65.2 us
  blocking collectives: 22.4 us -> 0 us
  local copies, waits for them, and re-layouts: 52.1 us -> 31.1 us
  between operations: 14.6 us -> 0.94 us
    reduce_scatter x1 -> x0, waiting for transfers between devices: 559 us -> none  [body(): lax.psum_scatter(jnp.einsum('th,td->hd', attn_flat, flat_cot, preferred_e...]
    pallas_call x0 -> x4, Pallas kernels: none -> 173 us  [the longest x2 105 us: exchange(): pl.pallas_call(functools.partial(exchange_kernel, len(arrays), forward),...]
    all_gather x1 -> x0, waiting for transfers between devices: 121 us -> none  [body(): weight_full = lax.all_gather(out_weight, ('seq', 'dp'), axis=0, tiled=True)]
    all_to_all x7 -> x0, waiting for transfers between devices: 63.5 us -> none  [the longest x1 13.8 us: body(): lax.all_to_all(column_query, 'seq', split_axis=2, concat_axis=1, tiled=True)]
    all_to_all x7 -> x0, starting transfers between devices: 37.2 us -> none  [the longest x1 9.22 us: body(): lax.all_to_all(column_query, 'seq', split_axis=2, concat_axis=1, tiled=True)]
    all_to_all x1 -> x0, blocking collectives: 22.4 us -> none  [body(): lax.all_to_all(column_upstream, 'seq', split_axis=2, concat_axis=1, tiled...]
  transfers between devices with their start and end apart: 9 -> 0, of which waited for: 8 -> 0; matrix products, arithmetic and copies ran while one was open for 7% -> 0% of each run, Pallas kernels for 0% -> 0%
where the time goes in v1:
time: 282 us
  Pallas kernels  173 us (61%)
  matrix products  65.2 us (23%)
  local copies, waits for them, and re-layouts  31.1 us (11%)
  other arithmetic  11.5 us (4%)
    pallas_call x2, Pallas kernels, exchange(): pl.pallas_call(functools.partial(exchange_kernel, len(arrays), forward),...  105 us
    pallas_call x1, Pallas kernels, summed_grad(): pl.pallas_call(functools.partial(scatter_kernel, factor), out_shape=jax.S...  34.7 us
    pallas_call x1, Pallas kernels, all_weight(): pl.pallas_call(gather_kernel, out_shape=jax.ShapeDtypeStruct((4, 4, 4, 16...  32.9 us
    dot_general x1, matrix products, body(): jnp.dot(attn, weight_full, preferred_element_type=jnp.float32)  9.42 us
    dot_general x5, matrix products, attend_sets(): jnp.einsum('...lm,...ld->...md', shares_low, upstream_set, preferred_elem...  8.26 us
    dot_general x1, matrix products, body(): jnp.einsum('td,hd->th', flat_cot, weight_full, preferred_element_type=jnp...  8.12 us
    dot_general x5, matrix products, attend_sets(): jnp.einsum('...ld,...md->...lm', upstream_set, value_set, preferred_eleme...  7.52 us
    dot_general x5, matrix products, attend_sets(): jnp.einsum('...lm,...md->...ld', score_low, key_set, preferred_element_ty...  6.85 us

profile of v1, /device:TPU:1, one launch (start us, length us, event | category | flops | bytes accessed | tf_op | source)
XLA Modules:
  0.0 281.6 jit_solution(5101578709924945330)
XLA Ops:
  0.7 3.3 %bitcast_bitcast_fusion.2 = (bf16[4,1024,128]{2,1,0:T(8,128)(2,1)}, bf16[4,1024,128]{2,1,0:T(8,128)(2,1)}) fusion(bf16[1024,1024]{1,0:T(8,128)(2,1)} %bitcast.202, bf16[1024,1024]{1,0:T(8,128)(2,1)} %bitcast.204), kind=kLoop, calls=%fused_computation.78 | loop fusion | bytes 4194304 | tf_op jit(solution)/shard_map/transpose | solution.py:361
  4.0 32.9 %shard_map.92 = bf16[4,4,4,16,2048]{4,3,2,1,0:T(8,128)(2,1)} custom-call(bf16[8,2048]{1,0:T(8,128)(2,1)} %w_ref.1), custom_call_target="tpu_custom_call" | custom-call | tf_op jit(solution)/shard_map/pallas_call | solution.py:263
  36.9 8.1 %fusion.49.refs_3_ = bf16[1024,1024]{1,0:T(8,128)(2,1)S(1)} fusion(bf16[1024,2048]{1,0:T(8,128)(2,1)} %bitcast.208, bf16[1,1,1024,2048]{3,2,1,0:T(8,128)(2,1)} %param.11), kind=kOutput, calls=%fused_computation.64 | convolution fusion | flops 4296015872 | bytes 10485760 | tf_op jit(solution)/shard_map/td,hd->th/dot_general | solution.py:348
  45.0 1.8 bitcast_bitcast_fusion
  48.4 34.9 %while.16 = (s32[]{:T(128)}, bf16[4,1024,128]{2,1,0:T(8,128)(2,1)S(1)}, bf16[4,1024,128]{2,1,0:T(8,128)(2,1)}, bf16[4,1024,128]{2,1,0:T(8,128)(2,1)}, bf16[4,102...) while((s32[]{:T(128)}, ...), condition=%wide.region_4.5_spmd, body=%wide.region_0.4_spmd.sunk | while | flops 1649144832 | bytes 51439780 | solution.py:358
  52.7 1.5 fusion.136
  55.6 1.5 fusion.138
  61.5 1.5 fusion.136
  64.3 1.5 fusion.138
  70.2 1.5 fusion.136
  73.1 1.5 fusion.138
  78.9 1.5 fusion.136
  80.4 1.5 fusion.137
  81.8 1.5 fusion.138
  84.5 55.0 %shard_map.93 = (bf16[32,32,512]{2,1,0:T(8,128)(2,1)}, bf16[32,32,512]{2,1,0:T(8,128)(2,1)}, bf16[32,32,512]{2,1,0:T(8,128)(2,1)}, bf16[32,32,512]{2,1,0:T(8,128)(2,1)}) custom-call(bf16[1024,1024]{1,0:T(8,128)(2,1)} %bitcast.203, bf16[1024,1024]{1,0:T(8,128)(2,1)} %bitcast.205, bf16[1024,1024]{1,0:T(8,128)(2,1)} %bitcast.206, bf16[1024,1024]{1,0:T(8,128)(2,1)} %copy-done.1), custom_call_target="tpu_custom_call" | custom-call | tf_op jit(solution)/shard_map/pallas_call | solution.py:297
  140.8 1.7 reshape.105
  143.9 3.2 %fusion.94 = (f32[32,4,32]{2,1,0:T(4,128)S(1)}, f32[32,4,32,32]{2,3,1,0:T(8,128)}) fusion(pred[32,32]{0,1:T(8,128)(4,1)S(1)} %iota_compare_fusion.1, bf16[32,32,4,128]{3,2,1,0:T(4,128)(2,1)S(1)} %reshape.105, bf16[32,32,4,128]{3,2,1,0:T(4,128)(2,1)S(1)} %reshape.104), kind=kOutput, calls=%fused_computation.112 | convolution fusion | flops 34078752 | bytes 2638848 | tf_op jit(solution)/shard_map/sub | solution.py:319
  147.2 2.5 fusion.53
  151.5 1.6 reshape.108
  153.1 4.0 %multiply_reduce_fusion.1 = (f32[32,4,32]{2,1,0:T(4,128)S(1)}, f32[32,4,32,32]{2,3,1,0:T(8,128)S(1)}) fusion(f32[32,4,32,32]{2,3,1,0:T(8,128)} %get-tuple-element.98, f32[32,4,32]{2,1,0:T(4,128)S(1)} %get-tuple-element.97, bf16[32,32,4,128]{3,2,1,0:T(4,128)(2,1)} %copy-done.6, bf16[32,32,4,128]{3,2,1,0:T(4,128)(2,1)S(1)} %reshape.108), kind=kOutput, calls=%fused_computation.61 | convolution fusion | flops 33943552 | bytes 3178496 | tf_op jit(solution)/shard_map/...ld,...md->...lm/dot_general | solution.py:325
  163.1 2.4 fusion.54
  167.3 50.1 %shard_map.94 = (bf16[1024,512]{1,0:T(8,128)(2,1)}, bf16[1024,512]{1,0:T(8,128)(2,1)}, bf16[1024,512]{1,0:T(8,128)(2,1)}, bf16[1024,512]{1,0:T(8,128)(2,1)}) custom-call(bf16[32,32,512]{2,1,0:T(8,128)(2,1)} %reshape.107.refs_0_, bf16[32,32,512]{2,1,0:T(8,128)(2,1)} %reshape.109.refs_1_, bf16[32,32,512]{2,1,0:T(8,128)(2,1)} %reshape.110.refs_2_, ...), custom_call_target="tpu_custom_call" | custom-call | tf_op jit(solution)/shard_map/pallas_call | solution.py:297
  217.4 2.4 constant_dynamic-update-slice_fusion
  219.8 9.4 %convert_bitcast_fusion = bf16[1,1,1024,2048]{3,2,1,0:T(8,128)(2,1)} fusion(bf16[1024,1024]{1,0:T(8,128)(2,1)} %constant_dynamic-update-slice_fusion, bf16[1024,2048]{1,0:T(8,128)(2,1)} %bitcast.209), kind=kOutput, calls=%fused_computation.53 | convolution fusion | flops 4297064448 | bytes 10485760 | tf_op jit(solution)/shard_map/dot_general | solution.py:369
  229.2 1.4 copy_bitcast_fusion.2
  230.7 1.6 maximum_bitcast_fusion
  233.7 1.6 maximum_bitcast_fusion.1
  235.3 1.5 copy_bitcast_fusion
  236.8 1.6 maximum_bitcast_fusion.2
  239.2 6.2 %fusion.46 = bf16[1024,2048]{1,0:T(8,128)(2,1)} fusion(bf16[1024,1024]{1,0:T(8,128)(2,1)S(1)} %copy-done.14, bf16[1,1,1024,2048]{3,2,1,0:T(8,128)(2,1)S(1)} %copy-done.15), kind=kOutput, calls=%fused_computation.54 | convolution fusion | flops 4297064448 | bytes 10485760 | tf_op jit(solution)/shard_map/th,td->hd/dot_general | solution.py:370
  245.4 34.7 %shard_map.95 = f32[8,2048]{1,0:T(8,128)} custom-call(bf16[4,4,4,16,2048]{4,3,2,1,0:T(8,128)(2,1)} %bitcast.210), custom_call_target="tpu_custom_call" | custom-call | tf_op jit(solution)/shard_map/pallas_call | solution.py:281
  280.1 1.5 copy.123
  (87 shorter events, 38.8 us)
Async XLA Ops:
  36.8 8.1 %copy-start = (bf16[1,1,1024,1024]{3,2,1,0:T(8,128)(2,1)S(1)}, bf16[1,1,1024,1024]{3,2,1,0:T(8,128)(2,1)}, u32[]{:S(2)}) copy-start(bf16[1,1,1024,1024]{3,2,1,0:T(8,128)(2,1)} %param.9) | copy-start | bytes 6291460
  45.0 2.1 copy-start.1
  45.0 2.1 copy-start.5
  45.0 3.0 %copy-start.7 = (bf16[4,1024,128]{2,1,0:T(8,128)(2,1)S(1)}, bf16[4,1024,128]{2,1,0:T(8,128)(2,1)}, u32[]{:S(2)}) copy-start(bf16[4,1024,128]{2,1,0:T(8,128)(2,1)} %get-tuple-element.174) | copy-start | bytes 3145732
  45.0 3.3 %copy-start.8 = (bf16[4,1024,128]{2,1,0:T(8,128)(2,1)S(1)}, bf16[4,1024,128]{2,1,0:T(8,128)(2,1)}, u32[]{:S(2)}) copy-start(bf16[4,1024,128]{2,1,0:T(8,128)(2,1)} %get-tuple-element.173) | copy-start | bytes 3145732
  48.4 1.2 copy-start.10
  49.6 1.2 copy-start.9
  57.1 1.2 copy-start.10
  58.4 1.2 copy-start.9
  65.8 1.2 copy-start.10
  67.0 1.2 copy-start.9
  74.5 1.2 copy-start.10
  75.8 1.2 copy-start.9
  140.8 6.3 %copy-start.6 = (bf16[32,32,4,128]{3,2,1,0:T(4,128)(2,1)}, bf16[32,32,4,128]{3,2,1,0:T(4,128)(2,1)S(1)}, u32[]{:S(2)}) copy-start(bf16[32,32,4,128]{3,2,1,0:T(4,128)(2,1)S(1)} %reshape.106) | copy-start | bytes 3145732
  153.0 4.0 %copy-start.3 = (bf16[32,32,4,128]{3,2,1,0:T(4,128)(2,1)}, bf16[32,32,4,128]{3,2,1,0:T(4,128)(2,1)S(1)}, u32[]{:S(2)}) copy-start(bf16[32,32,4,128]{3,2,1,0:T(4,128)(2,1)S(1)} %reshape.108) | copy-start | bytes 3145732
  153.1 4.0 %copy-start.2 = (f32[32,4,32,32]{2,3,1,0:T(8,128)S(1)}, f32[32,4,32,32]{2,3,1,0:T(8,128)}, u32[]{:S(2)}) copy-start(f32[32,4,32,32]{2,3,1,0:T(8,128)} %get-tuple-element.98) | copy-start | bytes 1572868
  161.3 1.8 copy-start.4
  219.8 10.9 %copy-start.13 = (bf16[1024,512]{1,0:T(8,128)(2,1)S(1)}, bf16[1024,512]{1,0:T(8,128)(2,1)}, u32[]{:S(2)}) copy-start(bf16[1024,512]{1,0:T(8,128)(2,1)} %get-tuple-element.70) | copy-start | bytes 3145732
  229.2 4.5 %copy-start.12 = (bf16[1024,512]{1,0:T(8,128)(2,1)S(1)}, bf16[1024,512]{1,0:T(8,128)(2,1)}, u32[]{:S(2)}) copy-start(bf16[1024,512]{1,0:T(8,128)(2,1)} %get-tuple-element.72) | copy-start | bytes 3145732
  232.3 4.5 %copy-start.11 = (bf16[1024,512]{1,0:T(8,128)(2,1)S(1)}, bf16[1024,512]{1,0:T(8,128)(2,1)}, u32[]{:S(2)}) copy-start(bf16[1024,512]{1,0:T(8,128)(2,1)} %get-tuple-element.74) | copy-start | bytes 3145732
  235.3 3.1 %copy-start.14 = (bf16[1024,1024]{1,0:T(8,128)(2,1)S(1)}, bf16[1024,1024]{1,0:T(8,128)(2,1)}, u32[]{:S(2)}) copy-start(bf16[1024,1024]{1,0:T(8,128)(2,1)} %constant_dynamic-update-slice_fusion) | copy-start | bytes 6291460
  235.3 3.9 %copy-start.15 = (bf16[1,1,1024,2048]{3,2,1,0:T(8,128)(2,1)S(1)}, bf16[1,1,1024,2048]{3,2,1,0:T(8,128)(2,1)}, u32[]{:S(2)}) copy-start(bf16[1,1,1024,2048]{3,2,1,0:T(8,128)(2,1)} %param.11) | copy-start | bytes 12582916

commit v2 on v1

v2 whole, which is shorter than its diff:
```python
import functools
import math

import jax
import jax.numpy as jnp
from jax import lax
from jax.experimental import pallas as pl
from jax.experimental.pallas import tpu as pltpu
from jax.sharding import PartitionSpec as P

ROW_HEADS = 4
COL_HEADS = 4
DH = 128
MESH = pl.DeviceIdType.MESH
VMEM_LIMIT = 67000000
PIECES = ((0, 384), (384, 384), (768, 256))
ORDERS = ((2, 1, 0), (1, 0, 2), (0, 2, 1))


def place():
    s = lax.axis_index("seq")
    p = lax.axis_index("dp")
    return (s // 8, (s // 2) % 4, (s % 2) * 2 + p // 2), p % 2


def device(at, core):
    y, x, z = at
    return ((y * 4 + x) * 2 + z // 2, (z % 2) * 2 + core)


def shifted(at, axis, step):
    moved = list(at)
    moved[axis] = (at[axis] + step) % 4
    return tuple(moved)


def greet(seq_peers, ring_peers):
    s = lax.axis_index("seq")
    p = lax.axis_index("dp")
    at, core = place()
    barrier = pltpu.get_barrier_semaphore()
    count = 0
    if seq_peers:

        @pl.loop(1, 32)
        def _(k):
            pl.semaphore_signal(
                barrier, inc=1, device_id=((s + k) % 32, p), device_id_type=MESH
            )

        count += 31
    if ring_peers:
        pl.semaphore_signal(barrier, inc=1, device_id=device(at, 1 - core), device_id_type=MESH)
        count += 1
        for axis in range(3):
            for step in range(1, 4):
                pl.semaphore_signal(
                    barrier,
                    inc=1,
                    device_id=device(shifted(at, axis, step), core),
                    device_id_type=MESH,
                )
                count += 1
    pl.semaphore_wait(barrier, count)


def remote(src, dst, send, recv, to):
    return pltpu.make_async_remote_copy(
        src_ref=src, dst_ref=dst, send_sem=send, recv_sem=recv, device_id=to, device_id_type=MESH
    )


def wait_bytes(ref, sem):
    pltpu.make_async_copy(ref, ref, sem).wait()


def gather_start(w_ref, pair, full, send, recv, local):
    at, core = place()
    swap = remote(w_ref, pair.at[core], send.at[0], recv.at[0], device(at, 1 - core))
    swap.start()
    own = pltpu.make_async_copy(w_ref, pair.at[core], local)
    own.start()
    own.wait()
    swap.wait()
    half = pl.ds(pl.multiple_of(core * 1024, 128), 1024)
    full[at[0], at[1], at[2], :, half] = jnp.concatenate(
        [pair[0, :, half], pair[1, :, half]], axis=0
    )


def gather_send(stage, full, send, recv):
    at, core = place()
    for k, ((start, width), order) in enumerate(zip(PIECES, ORDERS)):
        index = tuple(pl.ds(0, 4) if axis in order[:stage] else at[axis] for axis in range(3))
        cols = pl.ds(pl.multiple_of(core * 1024 + start, 128), width)
        region = full.at[index + (slice(None), cols)]
        for step in range(1, 4):
            to = device(shifted(at, order[stage], step), core)
            sem = 1 + 3 * stage + k
            remote(region, region, send.at[sem], recv.at[sem], to).start()


def gather_wait(stage, full, sems):
    at, core = place()
    for k, ((start, width), order) in enumerate(zip(PIECES, ORDERS)):
        index = tuple(
            pl.ds(0, 3)
            if axis == order[stage]
            else (pl.ds(0, 4) if axis in order[:stage] else at[axis])
            for axis in range(3)
        )
        wait_bytes(full.at[index + (slice(None), pl.ds(0, width))], sems.at[1 + 3 * stage + k])


def gather_last(full, send, recv):
    at, core = place()
    mine = full.at[:, :, :, :, pl.ds(pl.multiple_of(core * 1024, 128), 1024)]
    return remote(mine, mine, send.at[10], recv.at[10], device(at, 1 - core))


def scatter_grad(g_ref, out_ref, bufs, send, recv, factor, meanwhile):
    chip, firsts, seconds, thirds, sums1, sums2, fin, rest = bufs
    at, core = place()
    other = device(at, 1 - core)
    mine = pl.ds(pl.multiple_of(core * 1024, 128), 1024)
    theirs = pl.ds(pl.multiple_of((1 - core) * 1024, 128), 1024)
    swap = remote(g_ref.at[:, :, :, :, theirs], chip, send.at[0], recv.at[0], other)
    swap.start()
    swap.wait_recv()

    @pl.loop(0, 4)
    def _(y):
        @pl.loop(0, 4)
        def _(x):
            total = chip[y, x].astype(jnp.float32) + g_ref[y, x, :, :, mine].astype(jnp.float32)
            chip[y, x] = total.astype(jnp.bfloat16)

    sem = 1
    for stage in range(3):
        for k, ((start, width), order) in enumerate(zip(PIECES, ORDERS)):
            path = order[::-1]
            axis = path[stage]
            left = [a for a in range(3) if a not in path[:stage]]
            for step in range(1, 4):
                to = shifted(at, axis, step)
                index = tuple(to[a] if a == axis else slice(None) for a in left)
                if stage == 0:
                    src = chip.at[index + (slice(None), pl.ds(start, width))]
                    dst = firsts[k].at[step - 1]
                elif stage == 1:
                    src = sums1[k].at[index]
                    dst = seconds[k].at[step - 1]
                else:
                    src = sums2[k].at[index]
                    dst = thirds[k].at[step - 1]
                remote(src, dst, send.at[sem], recv.at[sem], device(to, core)).start()
            sem += 1
        if stage == 0:
            meanwhile()
            swap.wait_send()
        for k, ((start, width), order) in enumerate(zip(PIECES, ORDERS)):
            path = order[::-1]
            axis = path[stage]
            left = [a for a in range(3) if a not in path[:stage]]
            index = tuple(at[a] if a == axis else slice(None) for a in left)
            got = (firsts, seconds, thirds)[stage][k]
            wait_bytes(got, recv.at[sem - 3 + k])
            wait_bytes(got, send.at[sem - 3 + k])
            if stage == 0:
                own = chip[index + (slice(None), pl.ds(start, width))]
            elif stage == 1:
                own = sums1[k][index]
            else:
                own = sums2[k][index]
            total = own.astype(jnp.float32)
            for step in range(3):
                total = total + got[step].astype(jnp.float32)
            if stage == 0:
                sums1[k][...] = total.astype(jnp.bfloat16)
            elif stage == 1:
                sums2[k][...] = total.astype(jnp.bfloat16)
            else:
                for low in range(2):
                    fin[low, :, pl.ds(start, width)] = total[low * 8 : low * 8 + 8] * factor
    last = remote(fin.at[1 - core], rest, send.at[sem], recv.at[sem], other)
    last.start()
    last.wait()
    out_ref[:, mine] = fin[core]
    out_ref[:, theirs] = rest[...]


def scatter_bufs():
    def three(*lead):
        return [pltpu.VMEM(lead + (width,), jnp.bfloat16) for _, width in PIECES]

    return [
        pltpu.VMEM((4, 4, 4, 16, 1024), jnp.bfloat16),
        three(3, 4, 4, 16),
        three(3, 4, 16),
        three(3, 16),
        three(4, 4, 16),
        three(4, 16),
        pltpu.VMEM((2, 8, 1024), jnp.float32),
        pltpu.VMEM((8, 1024), jnp.float32),
    ]


def scatter_bufs():
    def three(*lead):
        return [pltpu.VMEM(lead + (width,), jnp.bfloat16) for _, width in PIECES]

    return [
        pltpu.VMEM((4, 4, 4, 16, 1024), jnp.bfloat16),
        three(3, 4, 4, 16),
        three(3, 4, 16),
        three(3, 16),
        three(4, 4, 16),
        three(4, 16),
        pltpu.VMEM((2, 8, 1024), jnp.float32),
        pltpu.VMEM((8, 1024), jnp.float32),
    ]


SCALE = 1.0 / math.sqrt(DH)
EXP2_SCALE = SCALE * math.log2(math.e)


def dot(a, b):
    return jnp.dot(a, b, preferred_element_type=jnp.float32)


def dot_nt(a, b):
    return lax.dot_general(a, b, (((1,), (1,)), ((), ())), preferred_element_type=jnp.float32)


def low(a):
    return a.astype(jnp.bfloat16)


def softmax_blocks(query, key_blocks, biases):
    scores = [dot_nt(key, query) for key in key_blocks]
    scores = [s if b is None else s + b for s, b in zip(scores, biases)]
    peak = functools.reduce(
        jnp.maximum, [jnp.max(s, axis=0, keepdims=True) for s in scores]
    )
    raised = [jnp.exp2((s - peak) * EXP2_SCALE) for s in scores]
    inverse = 1.0 / sum(jnp.sum(r, axis=0, keepdims=True) for r in raised)
    return [r * inverse for r in raised]


def score_grads(shares, value_blocks, upstream):
    grads = [dot_nt(value, upstream) for value in value_blocks]
    total = sum(jnp.sum(s * g, axis=0, keepdims=True) for s, g in zip(shares, grads))
    return [low(s * (g - total)) for s, g in zip(shares, grads)]


def row_head(head, qr, kr, vr, ur, attn, attn_t, dq, dk, dv, bias, key_t, value_t, dk_acc, dv_acc):
    lanes = pl.ds(pl.multiple_of(head * DH, DH), DH)
    key_t[...] = kr[:, lanes].T
    value_t[...] = vr[:, lanes].T
    for i in range(4):
        here = pl.ds(i * 256, 256)
        query, upstream = qr[here, lanes], ur[here, lanes]
        spans = [pl.ds(j * 256, 256) for j in range(i + 1)]
        shares = softmax_blocks(
            query, [kr[span, lanes] for span in spans], [None] * i + [bias[0]]
        )
        lows = [low(share) for share in shares]
        out_t = low(sum(dot(value_t[:, span], share) for span, share in zip(spans, lows)))
        attn_t[pl.ds(pl.multiple_of(head * DH, DH), DH), here] = out_t
        attn[here, lanes] = out_t.T
        grads = score_grads(shares, [vr[span, lanes] for span in spans], upstream)
        for j, span in enumerate(spans):
            to_value, to_key = dot(lows[j], upstream), dot(grads[j], query)
            if j == i:
                dv_acc[span] = to_value
                dk_acc[span] = to_key
            else:
                dv_acc[span] += to_value
                dk_acc[span] += to_key
        to_query = sum(dot(key_t[:, span], grad) for span, grad in zip(spans, grads))
        dq[here, lanes] = low(to_query.T * SCALE)
    dk[:, lanes] = low(dk_acc[...] * SCALE)
    dv[:, lanes] = low(dv_acc[...])


def column_block(ref, half, group, lanes):
    return ref[pl.ds(half * 16, 16), pl.ds(group, 16), lanes].reshape(256, DH)


def put_column(ref, half, group, lanes, block):
    ref[pl.ds(half * 16, 16), pl.ds(group, 16), lanes] = low(block).reshape(16, 16, DH)


def column_place(unit):
    group = pl.multiple_of((unit // 4) * 16, 16)
    return group, pl.ds(pl.multiple_of((unit % 4) * DH, DH), DH)


def column_forward(unit, cin, cout, bias, kept):
    group, lanes = column_place(unit)
    key = [column_block(cin[1], half, group, lanes) for half in range(2)]
    value_t = [column_block(cin[2], half, group, lanes).T for half in range(2)]
    slot = 0
    for i in range(2):
        query = column_block(cin[0], i, group, lanes)
        shares = softmax_blocks(query, key[: i + 1], [bias[1]] * i + [bias[2]])
        for share in shares:
            kept[unit, slot] = share
            slot += 1
        out_t = sum(dot(value_t[j], low(share)) for j, share in enumerate(shares))
        put_column(cout[0], i, group, lanes, out_t.T)


def column_backward(unit, cin, cout, kept):
    group, lanes = column_place(unit)
    key = [column_block(cin[1], half, group, lanes) for half in range(2)]
    key_t = [block.T for block in key]
    value = [column_block(cin[2], half, group, lanes) for half in range(2)]
    to_key, to_value = [0.0, 0.0], [0.0, 0.0]
    slot = 0
    for i in range(2):
        query = column_block(cin[0], i, group, lanes)
        upstream = column_block(cin[3], i, group, lanes)
        shares = [kept[unit, slot + j] for j in range(i + 1)]
        slot += i + 1
        grads = score_grads(shares, value[: i + 1], upstream)
        for j in range(i + 1):
            to_value[j] = to_value[j] + dot(low(shares[j]), upstream)
            to_key[j] = to_key[j] + dot(grads[j], query)
        to_query = sum(dot(key_t[j], grad) for j, grad in enumerate(grads))
        put_column(cout[1], i, group, lanes, to_query.T * SCALE)
    for j in range(2):
        put_column(cout[2], j, group, lanes, to_key[j] * SCALE)
        put_column(cout[3], j, group, lanes, to_value[j])


def mega_kernel(factor, *refs):
    q_in, k_in, v_in, w_in, cot_in = refs[:5]
    out_hbm, dq_hbm, dk_hbm, dv_hbm, grad_out = refs[5:10]
    (
        pair,
        full,
        cot,
        rows_in,
        u_row,
        u_col,
        cin,
        cout,
        attn,
        attn_t,
        rows_out,
        accs,
        trans,
        grad,
        layer,
        bias,
        kept,
        bufs,
        ag_send,
        ag_recv,
        rs_send,
        rs_recv,
        go_send,
        go_recv,
        go_local,
        back_send,
        back_recv,
        back_local,
        load,
        store,
    ) = refs[10:]
    s = lax.axis_index("seq")
    p = lax.axis_index("dp")
    row_half, col_half = pl.ds(0, 512), pl.ds(512, 512)
    loads = [pltpu.make_async_copy(cot_in, cot, load.at[0])] + [
        pltpu.make_async_copy(src.at[:, row_half], dst, load.at[1 + t])
        for t, (src, dst) in enumerate(zip((q_in, k_in, v_in), rows_in))
    ]
    for copy in loads:
        copy.start()

    def go_src(t, to):
        if t == 3:
            return u_col.at[pl.ds(to * 32, 32)]
        return (q_in, k_in, v_in)[t].at[pl.ds(to * 32, 32), col_half]

    def go_start(t):
        @pl.loop(1, 32)
        def _(k):
            to = (s + k) % 32
            remote(go_src(t, to), cin[t].at[s], go_send.at[t], go_recv.at[t], (to, p)).start()

        pltpu.make_async_copy(go_src(t, s), cin[t].at[s], go_local.at[t]).start()

    def go_wait(t):
        pltpu.make_async_copy(go_src(t, s), cin[t].at[s], go_local.at[t]).wait()
        wait_bytes(cin[t].at[pl.ds(0, 31)], go_recv.at[t])

    def back_dst(t):
        whole = (attn, dq_hbm, dk_hbm, dv_hbm)[t]
        return whole.at[pl.ds(s * 32, 32), col_half]

    def back_start(t):
        @pl.loop(1, 32)
        def _(k):
            to = (s + k) % 32
            remote(cout[t].at[to], back_dst(t), back_send.at[t], back_recv.at[t], (to, p)).start()

        pltpu.make_async_copy(cout[t].at[s], back_dst(t), back_local.at[t]).start()

    def back_wait(t):
        pltpu.make_async_copy(cout[t].at[s], back_dst(t), back_local.at[t]).wait()
        wait_bytes(cout[t].at[pl.ds(0, 31)], back_recv.at[t])

    greet(True, True)
    gather_start(w_in, pair, full, ag_send, ag_recv, load.at[4])
    gather_send(0, full, ag_send, ag_recv)
    lane = lax.broadcasted_iota(jnp.int32, (256, 256), 1)
    sub = lax.broadcasted_iota(jnp.int32, (256, 256), 0)
    same = lane % 16 == sub % 16
    bias[0] = jnp.where(sub <= lane, 0.0, -jnp.inf)
    bias[1] = jnp.where(same, 0.0, -jnp.inf)
    bias[2] = jnp.where(same & (sub <= lane), 0.0, -jnp.inf)
    gather_wait(0, full, ag_recv)
    gather_send(1, full, ag_send, ag_recv)
    gather_wait(1, full, ag_recv)
    gather_send(2, full, ag_send, ag_recv)
    for t in (1, 0, 2):
        go_start(t)
    gather_wait(2, full, ag_recv)
    last = gather_last(full, ag_send, ag_recv)
    last.start()
    last.wait_recv()
    loads[0].wait()

    def upstream_part(y, dst):
        weight = full.at[y]
        place_at = (y % 2) * 256

        @pl.loop(0, 2)
        def _(block):
            here = pl.ds(pl.multiple_of(block * 512, 512), 512)
            dst[here, pl.ds(place_at, 256)] = low(
                dot_nt(cot[here, :], weight[...].reshape(256, 2048))
            )

    upstream_part(2, u_col)
    upstream_part(3, u_col)
    go_start(3)
    upstream_part(0, u_row)
    upstream_part(1, u_row)
    for copy in loads[1:]:
        copy.wait()

    def row_heads(first, end):
        @pl.loop(first, end)
        def _(head):
            row_head(head, *rows_in, u_row, attn, attn_t, *rows_out, bias, *trans, *accs)

    row_heads(0, 2)
    for t in range(3):
        go_wait(t)

    @pl.loop(0, 8)
    def _(unit):
        column_forward(unit, cin, cout, bias, kept)

    back_start(0)
    row_heads(2, 3)
    go_wait(3)

    @pl.loop(0, 8)
    def _(unit):
        column_backward(unit, cin, cout, kept)

    for t in (3, 2, 1):
        back_start(t)
    row_heads(3, 4)
    row_stores = [
        pltpu.make_async_copy(src, dst.at[:, row_half], store.at[t])
        for t, (src, dst) in enumerate(zip(rows_out, (dq_hbm, dk_hbm, dv_hbm)))
    ]
    for copy in row_stores:
        copy.start()

    def grad_part(half):
        @pl.loop(0, 8)
        def _(block):
            cols = pl.ds(pl.multiple_of(block * 256, 256), 256)
            part = dot(attn_t[pl.ds(half * 512, 512), :], cot[:, cols])
            grad[pl.ds(half * 2, 2), :, :, :, cols] = low(part).reshape(2, 4, 4, 16, 256)

    grad_part(0)
    back_wait(0)

    @pl.loop(0, 4)
    def _(block):
        here = pl.ds(pl.multiple_of(block * 256, 256), 256)
        attn_t[pl.ds(512, 512), here] = attn[here, col_half].T

    grad_part(1)

    def project():
        @pl.loop(0, 8)
        def _(block):
            cols = pl.ds(pl.multiple_of(block * 256, 256), 256)
            layer[:, cols] = low(dot(attn[...], full[:, :, :, :, cols].reshape(1024, 256)))
            pltpu.make_async_copy(layer.at[:, cols], out_hbm.at[:, cols], store.at[3]).start()

    scatter_grad(grad, grad_out, bufs, rs_send, rs_recv, factor, project)
    pltpu.make_async_copy(layer, out_hbm, store.at[3]).wait()
    for copy in row_stores:
        copy.wait()
    for stage in range(3):
        gather_wait(stage, full, ag_send)
    last.wait_send()
    for t in (3, 2, 1):
        back_wait(t)
    for t in range(4):
        wait_bytes(cout[t].at[pl.ds(0, 31)], back_send.at[t])
        wait_bytes(cin[t].at[pl.ds(0, 31)], go_send.at[t])


ANY = pl.BlockSpec(memory_space=pl.ANY)
INV = pl.BlockSpec(memory_space=pltpu.VMEM)


def body(queries, keys, values, out_weight, cotangent):
    def vmem(*shape, dtype=jnp.bfloat16):
        return pltpu.VMEM(shape, dtype)

    def dma(count):
        return pltpu.SemaphoreType.DMA((count,))

    half = [1024, 512]
    shapes = [(1024, 2048), (1024, 1024), (1024, 1024), (1024, 1024)]
    results = pl.pallas_call(
        functools.partial(mega_kernel, 1.0 / math.sqrt(4 * 32 * 1024)),
        out_shape=[jax.ShapeDtypeStruct(shape, jnp.bfloat16) for shape in shapes]
        + [jax.ShapeDtypeStruct((8, 2048), jnp.float32)],
        in_specs=[ANY] * 5,
        out_specs=[ANY] * 4 + [INV],
        scratch_shapes=[
            vmem(2, 8, 2048),
            vmem(4, 4, 4, 16, 2048),
            vmem(1024, 2048),
            [vmem(*half) for _ in range(3)],
            vmem(*half),
            vmem(*half),
            [vmem(32, 32, 512) for _ in range(4)],
            [vmem(32, 32, 512) for _ in range(4)],
            vmem(1024, 1024),
            vmem(1024, 1024),
            [vmem(*half) for _ in range(3)],
            [vmem(1024, DH, dtype=jnp.float32) for _ in range(2)],
            [vmem(DH, 1024) for _ in range(2)],
            vmem(4, 4, 4, 16, 2048),
            vmem(1024, 2048),
            vmem(3, 256, 256, dtype=jnp.float32),
            vmem(8, 3, 256, 256, dtype=jnp.float32),
            scatter_bufs(),
            dma(11),
            dma(11),
            dma(11),
            dma(11),
            dma(4),
            dma(4),
            dma(4),
            dma(4),
            dma(4),
            dma(4),
            dma(5),
            dma(4),
        ],
        compiler_params=pltpu.CompilerParams(
            collective_id=1, has_side_effects=True, vmem_limit_bytes=VMEM_LIMIT
        ),
    )(
        *[member.reshape(1024, 1024) for member in (queries, keys, values)],
        out_weight,
        cotangent.reshape(1024, 2048),
    )
    return (
        results[0].reshape(1, 1, 1024, 2048),
        results[1].reshape(1, 1, 1024, 1024),
        results[2].reshape(1, 1, 1024, 1024),
        results[3].reshape(1, 1, 1024, 1024),
        results[4],
    )


def solution(mesh):
    return jax.shard_map(
        body,
        mesh=mesh,
        in_specs=(
            P("dp", "seq", None, None),
            P("dp", "seq", None, None),
            P("dp", "seq", None, None),
            P(("seq", "dp"), None),
            P("dp", "seq", None, None),
        ),
        out_specs=(
            P("dp", "seq", None, None),
            P("dp", "seq", None, None),
            P("dp", "seq", None, None),
            P("dp", "seq", None, None),
            P(("seq", "dp"), None),
        ),
        check_vma=False,
    )
```

time: 282 us -> 168 us (0.60)
  matrix products: 65.2 us -> 0 us
  local copies, waits for them, and re-layouts: 31.1 us -> 11.6 us
  Pallas kernels: 173 us -> 155 us
  other arithmetic: 11.5 us -> 0 us
    dot_general x32 -> x0, matrix products: 62 us -> none  [the longest x1 9.42 us: body(): jnp.dot(attn, weight_full, preferred_element_type=jnp.float32)]
    pallas_call x4 -> x1, Pallas kernels: 173 us -> 155 us  [body(): pl.pallas_call(functools.partial(mega_kernel, 1.0 / math.sqrt(4 * 32 * 10...]
    reshape x11 -> x0, local copies, waits for them, and re-layouts: 15.2 us -> none  [the longest x4 5.97 us: body(): member.reshape(32, 32, 4, 128)]
    unnamed x30 -> x13, local copies, waits for them, and re-layouts: 5.08 us -> 11.6 us
    transpose x2 -> x0, local copies, waits for them, and re-layouts: 5.05 us -> none  [body(): jnp.moveaxis(member[:, :512].reshape(1024, 4, 128), 1, 0)]
    reshape x3 -> x0, other arithmetic: 4.74 us -> none  [the longest x1 1.58 us: body(): joined[1].reshape(1, 1, 1024, 1024)]
    convert_element_type x5 -> x0, other arithmetic: 4.64 us -> none  [attend_sets(): score_low = (shares * (share_grad - row_total)).astype(jnp.bfloat16)]
    sub x1 -> x0, matrix products: 3.23 us -> none  [attend_sets(): raised = jnp.exp(scores - peak_score)]
where the time goes in v2:
time: 168 us
  Pallas kernels  155 us (92%)
  local copies, waits for them, and re-layouts  11.6 us (7%)
    pallas_call x1, Pallas kernels, body(): pl.pallas_call(functools.partial(mega_kernel, 1.0 / math.sqrt(4 * 32 * 10...  155 us
    unnamed x13, local copies, waits for them, and re-layouts  11.6 us

profile of v2, /device:TPU:1, one launch (start us, length us, event | category | flops | bytes accessed | tf_op | source)
XLA Modules:
  0.0 167.6 jit_solution(9537831491833326479)
XLA Ops:
  0.6 155.4 %shard_map.92 = (bf16[1024,2048]{1,0:T(8,128)(2,1)}, bf16[1024,1024]{1,0:T(8,128)(2,1)}, bf16[1024,1024]{1,0:T(8,128)(2,1)}, bf16[1024,1024]{1,0:T(8,128)(2,1)}, f32[8,2048]{1,0:T(8,128)}) custom-call(bf16[1024,1024]{1,0:T(8,128)(2,1)} %bitcast.10, bf16[1024,1024]{1,0:T(8,128)(2,1)} %bitcast.11, bf16[1024,1024]{1,0:T(8,128)(2,1)} %bitcast.12, ...), custom_call_target="tpu_custom_call" | custom-call | tf_op jit(solution)/shard_map/pallas_call | solution.py:538
  156.0 0.0 copy-start.2
  156.1 4.9 %copy.15 = bf16[1,1,1024,2048]{3,2,1,0:T(8,128)(2,1)} copy(bf16[1,1,1024,2048]{3,2,1,0:T(8,128)(2,1)} %bitcast.9) | data formatting | bytes 8388608
  161.0 0.0 copy-done.2
  161.0 0.0 copy-start.1
  161.0 1.3 copy.16
  162.3 1.0 copy-done.1
  163.3 0.0 copy-start
  163.3 1.3 copy.17
  164.7 1.0 copy-done
  165.7 0.0 copy-start.3
  165.7 1.3 copy.18
  167.0 0.0 copy-done.3
  167.0 0.6 copy.19
Async XLA Ops:
  156.0 4.9 %copy-start.2 = (bf16[1024,1024]{1,0:T(8,128)(2,1)S(1)}, bf16[1024,1024]{1,0:T(8,128)(2,1)}, u32[]{:S(2)}) copy-start(bf16[1024,1024]{1,0:T(8,128)(2,1)} %get-tuple-element.11) | copy-start | bytes 6291460
  161.0 2.3 %copy-start.1 = (bf16[1024,1024]{1,0:T(8,128)(2,1)S(1)}, bf16[1024,1024]{1,0:T(8,128)(2,1)}, u32[]{:S(2)}) copy-start(bf16[1024,1024]{1,0:T(8,128)(2,1)} %get-tuple-element.12) | copy-start | bytes 6291460
  163.3 2.3 %copy-start = (bf16[1024,1024]{1,0:T(8,128)(2,1)S(1)}, bf16[1024,1024]{1,0:T(8,128)(2,1)}, u32[]{:S(2)}) copy-start(bf16[1024,1024]{1,0:T(8,128)(2,1)} %get-tuple-element.13) | copy-start | bytes 6291460
  165.7 1.3 copy-start.3

commit v3 on v2

--- a/solution.py
+++ b/solution.py
@@ -118,15 +118,21 @@
     return remote(mine, mine, send.at[10], recv.at[10], device(at, 1 - core))
 
 
+def swap_start(half, g_ref, chip, send, recv):
+    at, core = place()
+    rows = pl.ds(half * 2, 2)
+    theirs = pl.ds(pl.multiple_of((1 - core) * 1024, 128), 1024)
+    src = g_ref.at[rows, :, :, :, theirs]
+    remote(src, chip.at[rows], send.at[0], recv.at[0], device(at, 1 - core)).start()
+
+
 def scatter_grad(g_ref, out_ref, bufs, send, recv, factor, meanwhile):
     chip, firsts, seconds, thirds, sums1, sums2, fin, rest = bufs
     at, core = place()
     other = device(at, 1 - core)
     mine = pl.ds(pl.multiple_of(core * 1024, 128), 1024)
     theirs = pl.ds(pl.multiple_of((1 - core) * 1024, 128), 1024)
-    swap = remote(g_ref.at[:, :, :, :, theirs], chip, send.at[0], recv.at[0], other)
-    swap.start()
-    swap.wait_recv()
+    wait_bytes(chip, recv.at[0])
 
     @pl.loop(0, 4)
     def _(y):
@@ -155,9 +161,7 @@
                     dst = thirds[k].at[step - 1]
                 remote(src, dst, send.at[sem], recv.at[sem], device(to, core)).start()
             sem += 1
-        if stage == 0:
-            meanwhile()
-            swap.wait_send()
+        meanwhile(stage)
         for k, ((start, width), order) in enumerate(zip(PIECES, ORDERS)):
             path = order[::-1]
             axis = path[stage]
@@ -185,24 +189,9 @@
     last = remote(fin.at[1 - core], rest, send.at[sem], recv.at[sem], other)
     last.start()
     last.wait()
+    wait_bytes(chip, send.at[0])
     out_ref[:, mine] = fin[core]
     out_ref[:, theirs] = rest[...]
-
-
-def scatter_bufs():
-    def three(*lead):
-        return [pltpu.VMEM(lead + (width,), jnp.bfloat16) for _, width in PIECES]
-
-    return [
-        pltpu.VMEM((4, 4, 4, 16, 1024), jnp.bfloat16),
-        three(3, 4, 4, 16),
-        three(3, 4, 16),
-        three(3, 16),
-        three(4, 4, 16),
-        three(4, 16),
-        pltpu.VMEM((2, 8, 1024), jnp.float32),
-        pltpu.VMEM((8, 1024), jnp.float32),
-    ]
 
 
 def scatter_bufs():
@@ -401,13 +390,14 @@
         whole = (attn, dq_hbm, dk_hbm, dv_hbm)[t]
         return whole.at[pl.ds(s * 32, 32), col_half]
 
-    def back_start(t):
-        @pl.loop(1, 32)
+    def back_start(t, first=1, end=32):
+        @pl.loop(first, end)
         def _(k):
             to = (s + k) % 32
             remote(cout[t].at[to], back_dst(t), back_send.at[t], back_recv.at[t], (to, p)).start()
 
-        pltpu.make_async_copy(cout[t].at[s], back_dst(t), back_local.at[t]).start()
+        if first == 1:
+            pltpu.make_async_copy(cout[t].at[s], back_dst(t), back_local.at[t]).start()
 
     def back_wait(t):
         pltpu.make_async_copy(cout[t].at[s], back_dst(t), back_local.at[t]).wait()
@@ -416,6 +406,7 @@
     greet(True, True)
     gather_start(w_in, pair, full, ag_send, ag_recv, load.at[4])
     gather_send(0, full, ag_send, ag_recv)
+    go_start(1)
     lane = lax.broadcasted_iota(jnp.int32, (256, 256), 1)
     sub = lax.broadcasted_iota(jnp.int32, (256, 256), 0)
     same = lane % 16 == sub % 16
@@ -424,10 +415,10 @@
     bias[2] = jnp.where(same & (sub <= lane), 0.0, -jnp.inf)
     gather_wait(0, full, ag_recv)
     gather_send(1, full, ag_send, ag_recv)
+    go_start(0)
     gather_wait(1, full, ag_recv)
     gather_send(2, full, ag_send, ag_recv)
-    for t in (1, 0, 2):
-        go_start(t)
+    go_start(2)
     gather_wait(2, full, ag_recv)
     last = gather_last(full, ag_send, ag_recv)
     last.start()
@@ -458,7 +449,6 @@
         def _(head):
             row_head(head, *rows_in, u_row, attn, attn_t, *rows_out, bias, *trans, *accs)
 
-    row_heads(0, 2)
     for t in range(3):
         go_wait(t)
 
@@ -467,16 +457,15 @@
         column_forward(unit, cin, cout, bias, kept)
 
     back_start(0)
-    row_heads(2, 3)
+    row_heads(0, 2)
     go_wait(3)
 
     @pl.loop(0, 8)
     def _(unit):
         column_backward(unit, cin, cout, kept)
 
-    for t in (3, 2, 1):
-        back_start(t)
-    row_heads(3, 4)
+    back_start(3)
+    row_heads(2, 4)
     row_stores = [
         pltpu.make_async_copy(src, dst.at[:, row_half], store.at[t])
         for t, (src, dst) in enumerate(zip(rows_out, (dq_hbm, dk_hbm, dv_hbm)))
@@ -492,6 +481,7 @@
             grad[pl.ds(half * 2, 2), :, :, :, cols] = low(part).reshape(2, 4, 4, 16, 256)
 
     grad_part(0)
+    swap_start(0, grad, bufs[0], rs_send, rs_recv)
     back_wait(0)
 
     @pl.loop(0, 4)
@@ -500,15 +490,22 @@
         attn_t[pl.ds(512, 512), here] = attn[here, col_half].T
 
     grad_part(1)
-
-    def project():
+    swap_start(1, grad, bufs[0], rs_send, rs_recv)
+
+    def meanwhile(stage):
+        if stage > 0:
+            for t, first, end in (((2, 16, 32),), ((1, 1, 32),))[stage - 1]:
+                back_start(t, first, end)
+            return
+        back_start(2, 1, 16)
+
         @pl.loop(0, 8)
         def _(block):
             cols = pl.ds(pl.multiple_of(block * 256, 256), 256)
             layer[:, cols] = low(dot(attn[...], full[:, :, :, :, cols].reshape(1024, 256)))
             pltpu.make_async_copy(layer.at[:, cols], out_hbm.at[:, cols], store.at[3]).start()
 
-    scatter_grad(grad, grad_out, bufs, rs_send, rs_recv, factor, project)
+    scatter_grad(grad, grad_out, bufs, rs_send, rs_recv, factor, meanwhile)
     pltpu.make_async_copy(layer, out_hbm, store.at[3]).wait()
     for copy in row_stores:
         copy.wait()

time: 168 us -> 161 us (0.958)
  Pallas kernels: 155 us -> 147 us
    pallas_call x1, Pallas kernels: 155 us -> 147 us  [body(): pl.pallas_call(functools.partial(mega_kernel, 1.0 / math.sqrt(4 * 32 * 10...]
where the time goes in v3:
time: 161 us; the launch traced here: 159 us
  Pallas kernels  147 us (91%)
  local copies, waits for them, and re-layouts  11.6 us (7%)
    pallas_call x1, Pallas kernels, body(): pl.pallas_call(functools.partial(mega_kernel, 1.0 / math.sqrt(4 * 32 * 10...  147 us
    unnamed x13, local copies, waits for them, and re-layouts  11.6 us

profile of v3, /device:TPU:1, one launch (start us, length us, event | category | flops | bytes accessed | tf_op | source)
XLA Modules:
  0.0 159.3 jit_solution(11655772489285778766)
XLA Ops:
  0.6 147.0 %shard_map.92 = (bf16[1024,2048]{1,0:T(8,128)(2,1)}, bf16[1024,1024]{1,0:T(8,128)(2,1)}, bf16[1024,1024]{1,0:T(8,128)(2,1)}, bf16[1024,1024]{1,0:T(8,128)(2,1)}, f32[8,2048]{1,0:T(8,128)}) custom-call(bf16[1024,1024]{1,0:T(8,128)(2,1)} %bitcast.10, bf16[1024,1024]{1,0:T(8,128)(2,1)} %bitcast.11, bf16[1024,1024]{1,0:T(8,128)(2,1)} %bitcast.12, ...), custom_call_target="tpu_custom_call" | custom-call | tf_op jit(solution)/shard_map/pallas_call | solution.py:535
  147.7 0.0 copy-start.2
  147.7 4.9 %copy.15 = bf16[1,1,1024,2048]{3,2,1,0:T(8,128)(2,1)} copy(bf16[1,1,1024,2048]{3,2,1,0:T(8,128)(2,1)} %bitcast.9) | data formatting | bytes 8388608
  152.6 0.0 copy-done.2
  152.6 0.0 copy-start.1
  152.6 1.3 copy.16
  153.9 1.0 copy-done.1
  155.0 0.0 copy-start
  155.0 1.3 copy.17
  156.3 1.0 copy-done
  157.3 0.0 copy-start.3
  157.3 1.3 copy.18
  158.6 0.0 copy-done.3
  158.6 0.6 copy.19
Async XLA Ops:
  147.7 4.9 %copy-start.2 = (bf16[1024,1024]{1,0:T(8,128)(2,1)S(1)}, bf16[1024,1024]{1,0:T(8,128)(2,1)}, u32[]{:S(2)}) copy-start(bf16[1024,1024]{1,0:T(8,128)(2,1)} %get-tuple-element.11) | copy-start | bytes 6291460
  152.6 2.3 %copy-start.1 = (bf16[1024,1024]{1,0:T(8,128)(2,1)S(1)}, bf16[1024,1024]{1,0:T(8,128)(2,1)}, u32[]{:S(2)}) copy-start(bf16[1024,1024]{1,0:T(8,128)(2,1)} %get-tuple-element.12) | copy-start | bytes 6291460
  155.0 2.3 %copy-start = (bf16[1024,1024]{1,0:T(8,128)(2,1)S(1)}, bf16[1024,1024]{1,0:T(8,128)(2,1)}, u32[]{:S(2)}) copy-start(bf16[1024,1024]{1,0:T(8,128)(2,1)} %get-tuple-element.13) | copy-start | bytes 6291460
  157.3 1.3 copy-start.3

commit v4 on v3

--- a/solution.py
+++ b/solution.py
@@ -523,6 +523,45 @@
 INV = pl.BlockSpec(memory_space=pltpu.VMEM)
 
 
+def settle_kernel(*refs):
+    srcs, dsts, held = refs[:5], refs[5:10], refs[10:15]
+    came, left = refs[15:]
+    chunks = []
+    for t, src in enumerate(srcs):
+        count = src.shape[0]
+        step = min(count, 256)
+        for start in range(0, count, step):
+            chunks.append((t, pl.ds(start, step)))
+    ins = [
+        pltpu.make_async_copy(srcs[t].at[rows], held[t].at[rows], came.at[n])
+        for n, (t, rows) in enumerate(chunks)
+    ]
+    outs = [
+        pltpu.make_async_copy(held[t].at[rows], dsts[t].at[rows], left.at[n])
+        for n, (t, rows) in enumerate(chunks)
+    ]
+    for copy in ins:
+        copy.start()
+    for coming, going in zip(ins, outs):
+        coming.wait()
+        going.start()
+    for copy in outs:
+        copy.wait()
+
+
+def settle(arrays):
+    shapes = [jax.ShapeDtypeStruct(member.shape, member.dtype) for member in arrays]
+    return pl.pallas_call(
+        settle_kernel,
+        out_shape=shapes,
+        in_specs=[ANY] * 5,
+        out_specs=[ANY] * 5,
+        scratch_shapes=[pltpu.VMEM(shape.shape, shape.dtype) for shape in shapes]
+        + [pltpu.SemaphoreType.DMA((17,))] * 2,
+        compiler_params=pltpu.CompilerParams(vmem_limit_bytes=VMEM_LIMIT),
+    )(*arrays)
+
+
 def body(queries, keys, values, out_weight, cotangent):
     def vmem(*shape, dtype=jnp.bfloat16):
         return pltpu.VMEM(shape, dtype)
@@ -578,6 +617,7 @@
         out_weight,
         cotangent.reshape(1024, 2048),
     )
+    results = settle(results)
     return (
         results[0].reshape(1, 1, 1024, 2048),
         results[1].reshape(1, 1, 1024, 1024),

time: 161 us -> 157 us (0.975)
  local copies, waits for them, and re-layouts: 11.6 us -> 0 us
  Pallas kernels: 147 us -> 155 us
    unnamed x13 -> x0, local copies, waits for them, and re-layouts: 11.6 us -> none
    pallas_call x0 -> x1, Pallas kernels: none -> 8.14 us  [settle(): pl.pallas_call(settle_kernel, out_shape=shapes, in_specs=[ANY] * 5, out_s...]
where the time goes in v4:
time: 157 us; the launch traced here: 156 us
  Pallas kernels  155 us (99%)
    pallas_call x1, Pallas kernels, body(): pl.pallas_call(functools.partial(mega_kernel, 1.0 / math.sqrt(4 * 32 * 10...  147 us
    pallas_call x1, Pallas kernels, settle(): pl.pallas_call(settle_kernel, out_shape=shapes, in_specs=[ANY] * 5, out_s...  8.14 us

profile of v4, /device:TPU:1, one launch (start us, length us, event | category | flops | bytes accessed | tf_op | source)
XLA Modules:
  0.0 155.8 jit_solution(13807526352612799074)
XLA Ops:
  0.6 147.0 %shard_map.92 = (bf16[1024,2048]{1,0:T(8,128)(2,1)}, bf16[1024,1024]{1,0:T(8,128)(2,1)}, bf16[1024,1024]{1,0:T(8,128)(2,1)}, bf16[1024,1024]{1,0:T(8,128)(2,1)}, f32[8,2048]{1,0:T(8,128)}) custom-call(bf16[1024,1024]{1,0:T(8,128)(2,1)} %bitcast.9, bf16[1024,1024]{1,0:T(8,128)(2,1)} %bitcast.10, bf16[1024,1024]{1,0:T(8,128)(2,1)} %bitcast.11, ...), custom_call_target="tpu_custom_call" | custom-call | tf_op jit(solution)/shard_map/pallas_call | solution.py:574
  147.7 8.1 %shard_map.93 = (bf16[1024,2048]{1,0:T(8,128)(2,1)}, bf16[1024,1024]{1,0:T(8,128)(2,1)}, bf16[1024,1024]{1,0:T(8,128)(2,1)}, bf16[1024,1024]{1,0:T(8,128)(2,1)}, f32[8,2048]{1,0:T(8,128)}) custom-call(bf16[1024,2048]{1,0:T(8,128)(2,1)} %get-tuple-element.15.refs_0_, bf16[1024,1024]{1,0:T(8,128)(2,1)} %get-tuple-element.16.refs_1_, ...), custom_call_target="tpu_custom_call" | custom-call | tf_op jit(solution)/shard_map/pallas_call | solution.py:554
